TPU v7x, 32 devices: a whole 2x2x4 slice. The times are simulated.
32 devices in a mesh: space: 4 (over y, core), vel: 8 (over z, x).
Axes of the slice: x: 2, y: 2, z: 4, core: 2. Of those that a mesh axis runs over, the one named last changes fastest.
Arguments:
- distribution: float32 [64, 48, 2304], P('space', 'vel'), may hold values from 0 to 2
- collision_rate: float32 [64], P('space'), may hold values from 0.1 to 1
- face_flags: int32 [64], replicated, may hold values 0 or 1
Outputs:
- updated: float32 [64, 48, 2304], P('space', 'vel')
All inputs are finite; a program needn't handle non-finite values.
Results may differ from a plain program's by a relative error of at most 0.0001.
Values sent between devices are 32-bit elements; how exact they have to be, the bound alone decides.
A program may use at most 64 MiB of HBM per device.

v0:
```python
import math
import jax
import jax.numpy as jnp
from jax import lax
from jax.sharding import PartitionSpec as P

NV = 48
LENGTH = 8.0
RADIUS = 6.0
COURANT = 0.9
GOLDEN = (1.0 + math.sqrt(5.0)) / 2.0
DIRECTIONS = (
    (0.0, 1.0, GOLDEN),
    (0.0, -1.0, GOLDEN),
    (1.0, GOLDEN, 0.0),
    (-1.0, GOLDEN, 0.0),
    (GOLDEN, 0.0, 1.0),
    (-GOLDEN, 0.0, 1.0),
)
HIGHEST_MODE = lax.Precision.HIGHEST


def padded_2(cells, sides, width):
    for axis, dim in sides:
        count = lax.axis_size(axis)
        ends = count - 1
        head = lax.slice_in_dim(cells, 0, width, axis=dim)
        tail = lax.slice_in_dim(cells, cells.shape[dim] - width, cells.shape[dim], axis=dim)
        cells = jnp.concatenate(
            [
                lax.ppermute(tail, axis, [(i, (i + 1) % count) for i in range(ends)]),
                cells,
                lax.ppermute(head, axis, [((i + 1) % count, i) for i in range(ends)]),
            ],
            axis=dim,
        )
    return cells


def kernel_tables(points):
    index = jnp.arange(points, dtype=jnp.int32)
    wrapped = jnp.where(
        index < points // 2, index, jnp.where(index == points // 2, 0, index - points)
    )
    signed = wrapped.astype(jnp.float32) * (math.pi / LENGTH)
    wave_x = signed[:, None, None]
    wave_y = signed[None, :, None]
    wave_z = signed[None, None, :]
    square = wave_x * wave_x + wave_y * wave_y + wave_z * wave_z
    scale = math.sqrt(1.0 + GOLDEN * GOLDEN)
    gain_tables = []
    loss_tables = []
    for direction in DIRECTIONS:
        parallel = (wave_x * direction[0] + wave_y * direction[1] + wave_z * direction[2]) / scale
        across = jnp.sqrt(jnp.maximum(square - parallel * parallel, 0.0))
        gain_tables.append(jnp.cos(0.5 * RADIUS * parallel))
        loss_tables.append(jnp.sinc(RADIUS * across / (2.0 * math.pi)))
    loss_total = sum(loss_tables) / 6.0
    return (gain_tables, loss_tables, loss_total)


def dft_tables(points):
    index = jnp.arange(points, dtype=jnp.int32)
    product = index[:, None] * index[None, :] % points
    angle = product.astype(jnp.float32) * (2.0 * math.pi / points)
    cosine = jnp.cos(angle)
    sine = jnp.sin(angle)
    first_table = jnp.stack([cosine, -sine], axis=1)
    forward_table = jnp.stack(
        [jnp.stack([cosine, -sine], axis=1), jnp.stack([sine, cosine], axis=1)], axis=1
    )
    inverse_table = jnp.stack(
        [jnp.stack([cosine, sine], axis=1), jnp.stack([-sine, cosine], axis=1)], axis=1
    )
    return (first_table, forward_table, inverse_table)


def apply_table(tensor, table, dims):
    return lax.dot_general(
        tensor,
        table,
        ((dims, tuple(range(len(dims)))), ((), ())),
        precision=HIGHEST_MODE,
        preferred_element_type=jnp.float32,
    )


def forward_cube(cube, tables):
    first_table, forward_table, inverse_table = tables
    section_one = apply_table(cube, first_table, (1,))
    section_two = apply_table(section_one, forward_table, (1, 2))
    return apply_table(section_two, forward_table, (0, 2))


def inverse_pair(spectrum, tables):
    first_table, forward_table, inverse_table = tables
    points = spectrum.shape[0]
    section_one = apply_table(spectrum, inverse_table, (3, 2))
    section_two = apply_table(section_one, inverse_table, (0, 2))
    section_three = apply_table(section_two, inverse_table, (0, 2))
    section_three = section_three * (1.0 / float(points**3))
    return (section_three[:, :, 0, :], section_three[:, :, 1, :])


def packed(spectrum, first_factor, second_factor):
    real_part = spectrum[:, :, 0, :]
    imag_part = spectrum[:, :, 1, :]
    first_factor = jnp.asarray(first_factor, jnp.float32)
    first_factor = first_factor[:, :, :] if first_factor.ndim == 3 else first_factor
    joined_real = first_factor * real_part - second_factor * imag_part
    joined_imag = first_factor * imag_part + second_factor * real_part
    return jnp.stack([joined_real, joined_imag], axis=2)


def collide(spectrum, kernels, tables):
    gain_tables, loss_tables, loss_total = kernels
    products = []
    for gain_table, loss_table in zip(gain_tables, loss_tables):
        first_part, second_part = inverse_pair(packed(spectrum, gain_table, loss_table), tables)
        products.append(first_part * second_part)
    gain_total = sum(products) / 6.0
    cube, loss_field = inverse_pair(packed(spectrum, 1.0, loss_total), tables)
    return gain_total - cube * loss_field


def body(distribution, collision_rate, face_flags):
    cell_count, planes_dev, width = distribution.shape
    points = NV
    tables = dft_tables(points)
    kernels = kernel_tables(points)

    def from_cell(one_cell):
        cube = one_cell.reshape(points, points, points)
        spectrum = forward_cube(cube, tables)
        return collide(spectrum, kernels, tables).reshape(points, width)

    regrouped = lax.all_to_all(distribution, "vel", split_axis=0, concat_axis=1, tiled=True)
    cell_terms = lax.map(from_cell, regrouped)
    collision_term = lax.all_to_all(cell_terms, "vel", split_axis=1, concat_axis=0, tiled=True)
    offset = lax.axis_index("space") * cell_count
    padded = padded_2(distribution, (("space", 0),), 1)
    mirror = distribution.reshape(cell_count, planes_dev, points, points)[:, :, ::-1, :].reshape(
        cell_count, planes_dev, width
    )
    wall_flags = jnp.concatenate([face_flags, jnp.ones((1,), jnp.int32)])
    nearby_walls = lax.dynamic_slice_in_dim(wall_flags, offset, cell_count + 1)
    lower_wall = (nearby_walls[:-1] == 1)[:, None, None]
    upper_wall = (nearby_walls[1:] == 1)[:, None, None]
    at_start = (offset + jnp.arange(cell_count, dtype=jnp.int32) == 0)[:, None, None]
    lower_side = jnp.where(lower_wall, mirror, jnp.where(at_start, distribution, padded[:-2]))
    upper_side = jnp.where(upper_wall, mirror, padded[2:])
    column = (jnp.arange(width, dtype=jnp.int32) // points).astype(jnp.float32)
    centre = (points - 1) / 2.0
    speed = COURANT * (column - centre) / centre
    upwind_flux = jnp.where(
        speed > 0, speed * (distribution - lower_side), speed * (upper_side - distribution)
    )
    return distribution - upwind_flux + collision_rate[:, None, None] * collision_term


def solution(mesh):
    return jax.shard_map(
        body,
        mesh=mesh,
        in_specs=(P("space", "vel", None), P("space"), P()),
        out_specs=P("space", "vel", None),
        check_vma=False,
    )
```

profile of v0, /device:TPU:0, one launch (start us, length us, event | category | flops | bytes accessed | tf_op | source)
XLA Modules:
  0.0 418.8 jit_solution(5220611589307567298)
XLA Ops:
  2.8 7.3 %all-to-all-start = ((f32[16,6,2304]{2,1,0:T(8,128)}), f32[16,6,2304]{2,1,0:T(8,128)S(1)}, u32[]{:S(2)}, u32[]{:S(2)}) async-start(f32[16,6,2304]{2,1,0:T(8,128)} %copy.77), calls=%async_computation | async-start | bytes 2359296 | tf_op jit(solution)/shard_map/all_to_all | solution.py:137
  10.6 13.5 %add_multiply_fusion = (f32[48,48,48]{2,1,0:T(8,128)}, f32[48,48,48]{2,1,0:T(8,128)}, f32[48,48,48]{2,1,0:T(8,128)}, f32[48,48,48]{2,1,0:T(8,128)}, f32[48,48,48...) fusion(f32[48]{0:T(128)S(1)} %get-tuple-element.737, f32[48,48]{1,0:T(8,128)S(1)} %get-tuple-element.739, ...), kind=kLoop, calls=%fused_computation.329 | loop fusion | flops 26652672 | bytes 3161856 | tf_op jit(solution)/shard_map/div | solution.py:58
  24.2 14.4 %all-to-all-done = f32[16,6,2304]{2,1,0:T(8,128)S(1)} async-done(((f32[16,6,2304]{2,1,0:T(8,128)}), f32[16,6,2304]{2,1,0:T(8,128)S(1)}, u32[]{:S(2)}, u32[]{:S(2)}) %all-to-all-start) | async-done | bytes 884768 | tf_op jit(solution)/shard_map/all_to_all | solution.py:137
  39.3 347.2 %while.13 = (s32[]{:T(128)}, f32[2,48,2304]{2,0,1:T(2,128)}, f32[2,48,2304]{2,0,1:T(2,128)S(1)}, f32[48,2,48]{2,0,1:T(8,128)S(1)}, f32[48,2,2,48]{3,0,1,2:T(8,12...) while((s32[]{:T(128)}, f32[2,48,2304]{2,0,1:T(2,128)}, ...), condition=%wide.region_1.3_spmd.clone.clone.clone, body=%wide.region_0.2_spmd.clone.clone.clone.sunk | while | flops 5998288896 | bytes 128030208 | solution.py:138
  49.0 6.0 %fusion.365 = f32[48,48,2,48,1]{0,3,4,2,1:T(8,128)S(1)} fusion(f32[48,48,2,48,1]{1,0,2,4,3:T(8,128)} %copy.170, f32[48,2,2,48]{3,0,1,2:T(8,128)S(1)} %get-tuple-element.770), kind=kOutput, calls=%fused_computation.156.clone.1 | convolution fusion | flops 254803968 | bytes 1806336 | tf_op jit(solution)/shard_map/while/body/eval_jaxpr/dot_general | solution.py:79
  57.1 10.0 %fusion.367 = (f32[48,48,1,48]{3,1,2,0:T(8,128)}, f32[48,48,1,48]{3,1,2,0:T(8,128)}, f32[48,48,1,48]{3,1,2,0:T(8,128)S(1)}, f32[48,48,1,48]{3,1,2,0:T(8,128)S(1)...) fusion(f32[48,48,48]{2,1,0:T(8,128)S(1)} %copy-done.16, f32[48]{0:T(128)S(1)} %get-tuple-element.779, ...), kind=kLoop, calls=%fused_computation.117.clone.1 | loop fusion | flops 2211840 | bytes 4884672 | tf_op jit(solution)/shard_map/while/body/eval_jaxpr/sub | solution.py:110
  74.5 6.0 %fusion.381 = f32[48,48,2,48,1]{0,3,4,2,1:T(8,128)S(1)} fusion(f32[48,48,2,48,1]{0,1,2,4,3:T(8,128)} %copy.176, f32[48,2,2,48]{3,0,1,2:T(8,128)S(1)} %get-tuple-element.772), kind=kOutput, calls=%fused_computation.148.clone.1 | convolution fusion | flops 254803968 | bytes 1806336 | tf_op jit(solution)/shard_map/while/body/eval_jaxpr/dot_general | solution.py:79
  91.4 6.0 %fusion.383 = f32[48,48,2,48,1]{0,3,4,2,1:T(8,128)S(1)} fusion(f32[48,48,2,48,1]{0,1,2,4,3:T(8,128)} %copy.177, f32[48,2,2,48]{3,0,1,2:T(8,128)S(1)} %get-tuple-element.772), kind=kOutput, calls=%fused_computation.152.clone.1 | convolution fusion | flops 254803968 | bytes 1806336 | tf_op jit(solution)/shard_map/while/body/eval_jaxpr/dot_general | solution.py:79
  101.0 9.6 %fusion.370 = (f32[48,48,1,48]{3,1,2,0:T(8,128)}, f32[48,48,1,48]{3,1,2,0:T(8,128)}, f32[48,48,1,48]{3,1,2,0:T(8,128)S(1)}, f32[48,48,1,48]{3,1,2,0:T(8,128)S(1)}) fusion(f32[48,48,48]{2,1,0:T(8,128)S(1)} %copy-done.18, f32[48]{0:T(128)S(1)} %get-tuple-element.785, f32[48,48]{1,0:T(8,128)S(1)} %copy-done.24, f32[48,48,2,48]{3,1,2,0:T(8,128)S(1)} %fusion.366, ...), kind=kLoop, calls=%fused_computation.93.clone.1 | loop fusion | flops 1769472 | bytes 3557568 | tf_op jit(solution)/shard_map/while/body/eval_jaxpr/sub | solution.py:110
  118.0 6.0 %fusion.372 = f32[48,48,2,48,1]{0,3,4,2,1:T(8,128)S(1)} fusion(f32[48,48,2,48,1]{0,1,2,4,3:T(8,128)} %copy.172, f32[48,2,2,48]{3,0,1,2:T(8,128)S(1)} %get-tuple-element.772), kind=kOutput, calls=%fused_computation.132.clone.1 | convolution fusion | flops 254803968 | bytes 1806336 | tf_op jit(solution)/shard_map/while/body/eval_jaxpr/dot_general | solution.py:79
  131.0 4.1 copy.173
  135.2 6.0 %fusion.374 = f32[48,48,2,48,1]{0,3,4,2,1:T(8,128)S(1)} fusion(f32[48,48,2,48,1]{0,1,2,4,3:T(8,128)} %copy.173, f32[48,2,2,48]{3,0,1,2:T(8,128)S(1)} %get-tuple-element.772), kind=kOutput, calls=%fused_computation.136.clone.1 | convolution fusion | flops 254803968 | bytes 1806336 | tf_op jit(solution)/shard_map/while/body/eval_jaxpr/dot_general | solution.py:79
  144.8 9.6 %fusion.375 = (f32[48,48,1,48]{3,1,2,0:T(8,128)}, f32[48,48,1,48]{3,1,2,0:T(8,128)}, f32[48,48,1,48]{3,1,2,0:T(8,128)S(1)}, f32[48,48,1,48]{3,1,2,0:T(8,128)S(1)}) fusion(f32[48,48,48]{2,1,0:T(8,128)S(1)} %copy-done.14, f32[48]{0:T(128)S(1)} %get-tuple-element.782, f32[48,48]{1,0:T(8,128)S(1)} %copy-done.26, f32[48,48,2,48]{3,1,2,0:T(8,128)S(1)} %fusion.366, ...), kind=kLoop, calls=%fused_computation.105.clone.1 | loop fusion | flops 1769472 | bytes 3557568 | tf_op jit(solution)/shard_map/while/body/eval_jaxpr/sub | solution.py:110
  159.2 6.0 %fusion.377 = f32[48,48,2,48,1]{0,3,4,2,1:T(8,128)S(1)} fusion(f32[48,48,2,48,1]{0,1,2,4,3:T(8,128)} %copy.174, f32[48,2,2,48]{3,0,1,2:T(8,128)S(1)} %get-tuple-element.772), kind=kOutput, calls=%fused_computation.140.clone.1 | convolution fusion | flops 254803968 | bytes 1806336 | tf_op jit(solution)/shard_map/while/body/eval_jaxpr/dot_general | solution.py:79
  174.7 6.0 %fusion.379 = f32[48,48,2,48,1]{0,3,4,2,1:T(8,128)S(1)} fusion(f32[48,48,2,48,1]{0,1,2,4,3:T(8,128)} %copy.175, f32[48,2,2,48]{3,0,1,2:T(8,128)S(1)} %get-tuple-element.772), kind=kOutput, calls=%fused_computation.144.clone.1 | convolution fusion | flops 254803968 | bytes 1806336 | tf_op jit(solution)/shard_map/while/body/eval_jaxpr/dot_general | solution.py:79
  191.7 6.2 %fusion.369 = f32[48,48,2,48,1]{0,3,4,2,1:T(8,128)S(1)} fusion(f32[48,48,2,48,1]{0,1,2,4,3:T(8,128)} %copy.171, f32[48,2,2,48]{3,0,1,2:T(8,128)S(1)} %get-tuple-element.772), kind=kOutput, calls=%fused_computation.128.clone.1 | convolution fusion | flops 254803968 | bytes 1806336 | tf_op jit(solution)/shard_map/while/body/eval_jaxpr/dot_general | solution.py:79
  200.2 4.2 fusion.384
  220.4 6.0 %fusion.365 = f32[48,48,2,48,1]{0,3,4,2,1:T(8,128)S(1)} fusion(f32[48,48,2,48,1]{1,0,2,4,3:T(8,128)} %copy.170, f32[48,2,2,48]{3,0,1,2:T(8,128)S(1)} %get-tuple-element.770), kind=kOutput, calls=%fused_computation.156.clone.1 | convolution fusion | flops 254803968 | bytes 1806336 | tf_op jit(solution)/shard_map/while/body/eval_jaxpr/dot_general | solution.py:79
  228.6 10.0 %fusion.367 = (f32[48,48,1,48]{3,1,2,0:T(8,128)}, f32[48,48,1,48]{3,1,2,0:T(8,128)}, f32[48,48,1,48]{3,1,2,0:T(8,128)S(1)}, f32[48,48,1,48]{3,1,2,0:T(8,128)S(1)...) fusion(f32[48,48,48]{2,1,0:T(8,128)S(1)} %copy-done.16, f32[48]{0:T(128)S(1)} %get-tuple-element.779, ...), kind=kLoop, calls=%fused_computation.117.clone.1 | loop fusion | flops 2211840 | bytes 4884672 | tf_op jit(solution)/shard_map/while/body/eval_jaxpr/sub | solution.py:110
  246.0 6.0 %fusion.381 = f32[48,48,2,48,1]{0,3,4,2,1:T(8,128)S(1)} fusion(f32[48,48,2,48,1]{0,1,2,4,3:T(8,128)} %copy.176, f32[48,2,2,48]{3,0,1,2:T(8,128)S(1)} %get-tuple-element.772), kind=kOutput, calls=%fused_computation.148.clone.1 | convolution fusion | flops 254803968 | bytes 1806336 | tf_op jit(solution)/shard_map/while/body/eval_jaxpr/dot_general | solution.py:79
  262.9 6.0 %fusion.383 = f32[48,48,2,48,1]{0,3,4,2,1:T(8,128)S(1)} fusion(f32[48,48,2,48,1]{0,1,2,4,3:T(8,128)} %copy.177, f32[48,2,2,48]{3,0,1,2:T(8,128)S(1)} %get-tuple-element.772), kind=kOutput, calls=%fused_computation.152.clone.1 | convolution fusion | flops 254803968 | bytes 1806336 | tf_op jit(solution)/shard_map/while/body/eval_jaxpr/dot_general | solution.py:79
  272.5 9.6 %fusion.370 = (f32[48,48,1,48]{3,1,2,0:T(8,128)}, f32[48,48,1,48]{3,1,2,0:T(8,128)}, f32[48,48,1,48]{3,1,2,0:T(8,128)S(1)}, f32[48,48,1,48]{3,1,2,0:T(8,128)S(1)}) fusion(f32[48,48,48]{2,1,0:T(8,128)S(1)} %copy-done.18, f32[48]{0:T(128)S(1)} %get-tuple-element.785, f32[48,48]{1,0:T(8,128)S(1)} %copy-done.24, f32[48,48,2,48]{3,1,2,0:T(8,128)S(1)} %fusion.366, ...), kind=kLoop, calls=%fused_computation.93.clone.1 | loop fusion | flops 1769472 | bytes 3557568 | tf_op jit(solution)/shard_map/while/body/eval_jaxpr/sub | solution.py:110
  285.5 4.2 %copy.172 = f32[48,48,2,48,1]{0,1,2,4,3:T(8,128)} copy(f32[48,48,2,48,1]{3,1,2,0,4:T(8,128)} %fusion.371) | data formatting | bytes 1769472 | tf_op jit(solution)/shard_map/while/body/eval_jaxpr/dot_general | solution.py:79
  289.8 6.0 %fusion.372 = f32[48,48,2,48,1]{0,3,4,2,1:T(8,128)S(1)} fusion(f32[48,48,2,48,1]{0,1,2,4,3:T(8,128)} %copy.172, f32[48,2,2,48]{3,0,1,2:T(8,128)S(1)} %get-tuple-element.772), kind=kOutput, calls=%fused_computation.132.clone.1 | convolution fusion | flops 254803968 | bytes 1806336 | tf_op jit(solution)/shard_map/while/body/eval_jaxpr/dot_general | solution.py:79
  306.6 6.0 %fusion.374 = f32[48,48,2,48,1]{0,3,4,2,1:T(8,128)S(1)} fusion(f32[48,48,2,48,1]{0,1,2,4,3:T(8,128)} %copy.173, f32[48,2,2,48]{3,0,1,2:T(8,128)S(1)} %get-tuple-element.772), kind=kOutput, calls=%fused_computation.136.clone.1 | convolution fusion | flops 254803968 | bytes 1806336 | tf_op jit(solution)/shard_map/while/body/eval_jaxpr/dot_general | solution.py:79
  316.3 9.6 %fusion.375 = (f32[48,48,1,48]{3,1,2,0:T(8,128)}, f32[48,48,1,48]{3,1,2,0:T(8,128)}, f32[48,48,1,48]{3,1,2,0:T(8,128)S(1)}, f32[48,48,1,48]{3,1,2,0:T(8,128)S(1)}) fusion(f32[48,48,48]{2,1,0:T(8,128)S(1)} %copy-done.14, f32[48]{0:T(128)S(1)} %get-tuple-element.782, f32[48,48]{1,0:T(8,128)S(1)} %copy-done.26, f32[48,48,2,48]{3,1,2,0:T(8,128)S(1)} %fusion.366, ...), kind=kLoop, calls=%fused_computation.105.clone.1 | loop fusion | flops 1769472 | bytes 3557568 | tf_op jit(solution)/shard_map/while/body/eval_jaxpr/sub | solution.py:110
  330.7 6.0 %fusion.377 = f32[48,48,2,48,1]{0,3,4,2,1:T(8,128)S(1)} fusion(f32[48,48,2,48,1]{0,1,2,4,3:T(8,128)} %copy.174, f32[48,2,2,48]{3,0,1,2:T(8,128)S(1)} %get-tuple-element.772), kind=kOutput, calls=%fused_computation.140.clone.1 | convolution fusion | flops 254803968 | bytes 1806336 | tf_op jit(solution)/shard_map/while/body/eval_jaxpr/dot_general | solution.py:79
  346.3 6.0 %fusion.379 = f32[48,48,2,48,1]{0,3,4,2,1:T(8,128)S(1)} fusion(f32[48,48,2,48,1]{0,1,2,4,3:T(8,128)} %copy.175, f32[48,2,2,48]{3,0,1,2:T(8,128)S(1)} %get-tuple-element.772), kind=kOutput, calls=%fused_computation.144.clone.1 | convolution fusion | flops 254803968 | bytes 1806336 | tf_op jit(solution)/shard_map/while/body/eval_jaxpr/dot_general | solution.py:79
  363.3 6.2 %fusion.369 = f32[48,48,2,48,1]{0,3,4,2,1:T(8,128)S(1)} fusion(f32[48,48,2,48,1]{0,1,2,4,3:T(8,128)} %copy.171, f32[48,2,2,48]{3,0,1,2:T(8,128)S(1)} %get-tuple-element.772), kind=kOutput, calls=%fused_computation.128.clone.1 | convolution fusion | flops 254803968 | bytes 1806336 | tf_op jit(solution)/shard_map/while/body/eval_jaxpr/dot_general | solution.py:79
  371.8 4.2 fusion.384
  386.5 4.4 %all-to-all-start.1 = ((f32[2,48,2304]{2,0,1:T(2,128)}), f32[2,48,2304]{2,0,1:T(2,128)}, u32[]{:S(2)}, u32[]{:S(2)}) async-start(f32[2,48,2304]{2,0,1:T(2,128)} %get-tuple-element.142), calls=%async_computation.1 | async-start | bytes 1769472 | tf_op jit(solution)/shard_map/all_to_all | solution.py:139
  402.2 10.9 %all-to-all-done.1 = f32[2,48,2304]{2,0,1:T(2,128)} async-done(((f32[2,48,2304]{2,0,1:T(2,128)}), f32[2,48,2304]{2,0,1:T(2,128)}, u32[]{:S(2)}, u32[]{:S(2)}) %all-to-all-start.1) | async-done | bytes 884768 | tf_op jit(solution)/shard_map/all_to_all | solution.py:139
  (206 shorter events, 190.8 us)
Async XLA Ops:
  2.8 35.8 %all-to-all-start = ((f32[16,6,2304]{2,1,0:T(8,128)}), f32[16,6,2304]{2,1,0:T(8,128)S(1)}, u32[]{:S(2)}, u32[]{:S(2)}) async-start(f32[16,6,2304]{2,1,0:T(8,128)} %copy.77), calls=%async_computation | async-start | bytes 2359296 | tf_op jit(solution)/shard_map/all_to_all | solution.py:137
  10.0 14.1 %copy-start.31 = (f32[48]{0:T(128)}, f32[48]{0:T(128)S(1)}, u32[]{:S(2)}) copy-start(f32[48]{0:T(128)S(1)} %get-tuple-element.734) | copy-start | bytes 580
  10.6 13.6 %copy-start.21 = (f32[48,48]{1,0:T(8,128)}, f32[48,48]{1,0:T(8,128)S(1)}, u32[]{:S(2)}) copy-start(f32[48,48]{1,0:T(8,128)S(1)} %get-tuple-element.736) | copy-start | bytes 27652
  10.6 13.6 %copy-start.23 = (f32[48,48]{1,0:T(8,128)}, f32[48,48]{1,0:T(8,128)S(1)}, u32[]{:S(2)}) copy-start(f32[48,48]{1,0:T(8,128)S(1)} %get-tuple-element.738) | copy-start | bytes 27652
  10.6 13.6 %copy-start.25 = (f32[48,48]{1,0:T(8,128)}, f32[48,48]{1,0:T(8,128)S(1)}, u32[]{:S(2)}) copy-start(f32[48,48]{1,0:T(8,128)S(1)} %get-tuple-element.735) | copy-start | bytes 27652
  10.6 13.6 %copy-start.27 = (f32[48,48]{1,0:T(8,128)}, f32[48,48]{1,0:T(8,128)S(1)}, u32[]{:S(2)}) copy-start(f32[48,48]{1,0:T(8,128)S(1)} %get-tuple-element.732) | copy-start | bytes 27652
  80.5 3.5 copy-start.6
  80.5 3.5 copy-start.7
  97.4 3.6 copy-start.17
  97.4 3.5 copy-start.18
  97.4 3.5 copy-start.24
  141.2 3.6 copy-start.13
  141.2 3.6 copy-start.14
  141.2 3.6 copy-start.22
  141.2 3.6 copy-start.26
  191.7 8.3 %copy-start.2 = (f32[48,48,2,48]{3,1,2,0:T(8,128)S(1)}, f32[48,48,2,48]{3,1,2,0:T(8,128)}, u32[]{:S(2)}) copy-start(f32[48,48,2,48]{3,1,2,0:T(8,128)} %bitcast_multiply_fusion.41) | copy-start | bytes 2654212 | tf_op jit(solution)/shard_map/while
  191.7 8.3 %copy-start.3 = (f32[48,48,2,48]{3,1,2,0:T(8,128)S(1)}, f32[48,48,2,48]{3,1,2,0:T(8,128)}, u32[]{:S(2)}) copy-start(f32[48,48,2,48]{3,1,2,0:T(8,128)} %bitcast_multiply_fusion.42) | copy-start | bytes 2654212 | tf_op jit(solution)/shard_map/while
  252.0 3.5 copy-start.6
  268.9 3.6 copy-start.17
  269.0 3.5 copy-start.18
  269.0 3.5 copy-start.24
  312.7 3.6 copy-start.13
  312.7 3.6 copy-start.14
  312.7 3.6 copy-start.22
  312.7 3.6 copy-start.26
  363.3 8.3 %copy-start.2 = (f32[48,48,2,48]{3,1,2,0:T(8,128)S(1)}, f32[48,48,2,48]{3,1,2,0:T(8,128)}, u32[]{:S(2)}) copy-start(f32[48,48,2,48]{3,1,2,0:T(8,128)} %bitcast_multiply_fusion.41) | copy-start | bytes 2654212 | tf_op jit(solution)/shard_map/while
  363.3 8.3 %copy-start.3 = (f32[48,48,2,48]{3,1,2,0:T(8,128)S(1)}, f32[48,48,2,48]{3,1,2,0:T(8,128)}, u32[]{:S(2)}) copy-start(f32[48,48,2,48]{3,1,2,0:T(8,128)} %bitcast_multiply_fusion.42) | copy-start | bytes 2654212 | tf_op jit(solution)/shard_map/while
  386.5 4.4 %copy-start.19 = (f32[16,6,2304]{2,0,1:T(8,128)S(1)}, f32[16,6,2304]{2,0,1:T(8,128)}, u32[]{:S(2)}) copy-start(f32[16,6,2304]{2,0,1:T(8,128)} %param.6) | copy-start | bytes 2654212
  386.5 7.1 %copy-start.34 = (s32[64]{0:T(128)S(1)}, s32[64]{0:T(128)}, u32[]{:S(2)}) copy-start(s32[64]{0:T(128)} %param.8) | copy-start | bytes 772
  386.5 26.5 %all-to-all-start.1 = ((f32[2,48,2304]{2,0,1:T(2,128)}), f32[2,48,2304]{2,0,1:T(2,128)}, u32[]{:S(2)}, u32[]{:S(2)}) async-start(f32[2,48,2304]{2,0,1:T(2,128)} %get-tuple-element.142), calls=%async_computation.1 | async-start | bytes 1769472 | tf_op jit(solution)/shard_map/all_to_all | solution.py:139
  391.0 26.1 %collective-permute-start = (f32[1,6,2304]{2,0,1:T(1,128)S(1)}, f32[1,6,2304]{2,0,1:T(1,128)S(1)}, u32[]{:S(2)}, u32[]{:S(2)}) collective-permute-start(f32[1,6,2304]{2,0,1:T(1,128)S(1)} %get-tuple-element.523), channel_id=1, source_target_pairs={{0,8},{8,16},{16,24},{1,9},{9,17},{17,25},{2,10},{10,18},{18,26},{... | collective-permute-start | bytes 165896 | tf_op jit(solution)/shard_map/ppermute | solution.py:31
  392.3 24.9 %collective-permute-start.1 = (f32[1,6,2304]{2,0,1:T(1,128)S(1)}, f32[1,6,2304]{2,0,1:T(1,128)S(1)}, u32[]{:S(2)}, u32[]{:S(2)}) collective-permute-start(f32[1,6,2304]{2,0,1:T(1,128)S(1)} %get-tuple-element.524), channel_id=1, source_target_pairs={{8,0},{16,8},{24,16},{9,1},{17,9},{25,17},{10,2},{18,10},{26,18},{... | collective-permute-start | bytes 165896 | tf_op jit(solution)/shard_map/ppermute | solution.py:33
  (32 other events, 76.8 us)
where the time goes:
time: 423 us; the launch traced here: 419 us
  matrix products  196 us (46%)
  local copies, waits for them, and re-layouts  94.4 us (22%)
  other arithmetic  82.4 us (19%)
  waiting for transfers between devices  25.3 us (6%)
  starting transfers between devices  14.2 us (3%)
  loops' own time  5.61 us (1%)
    dot_general x48, matrix products, apply_table(): lax.dot_general(tensor, table, ((dims, tuple(range(len(dims)))), ((), ())...  196 us
    dot_general x16, local copies, waits for them, and re-layouts, apply_table(): lax.dot_general(tensor, table, ((dims, tuple(range(len(dims)))), ((), ())...  60.6 us
    sub x6, other arithmetic, packed(): joined_real = first_factor * real_part - second_factor * imag_part  58.4 us
    all_to_all x1, waiting for transfers between devices, body(): lax.all_to_all(distribution, 'vel', split_axis=0, concat_axis=1, tiled=True)  14.4 us
    div x1, other arithmetic, kernel_tables(): loss_total = sum(loss_tables) / 6.0  13.5 us
    all_to_all x1, waiting for transfers between devices, body(): lax.all_to_all(cell_terms, 'vel', split_axis=1, concat_axis=0, tiled=True)  10.9 us
  transfers between devices with their start and end apart: 4, of which 2 were waited for; matrix products, arithmetic and copies ran while one was open for 6% of the time, Pallas kernels for 0%

commit v1 on v0

--- a/solution.py
+++ b/solution.py
@@ -18,6 +18,18 @@
     (-GOLDEN, 0.0, 1.0),
 )
 HIGHEST_MODE = lax.Precision.HIGHEST
+
+
+def cut_along(x, dim, count):
+    shape = x.shape
+    pieces = x.reshape(*shape[:dim], count, shape[dim] // count, *shape[dim + 1 :])
+    return jnp.moveaxis(pieces, dim, 0)
+
+
+def laid_out(blocks, dim):
+    blocks = jnp.moveaxis(blocks, 0, dim)
+    shape = blocks.shape
+    return blocks.reshape(*shape[:dim], shape[dim] * shape[dim + 1], *shape[dim + 2 :])
 
 
 def padded_2(cells, sides, width):
@@ -136,7 +148,17 @@
 
     regrouped = lax.all_to_all(distribution, "vel", split_axis=0, concat_axis=1, tiled=True)
     cell_terms = lax.map(from_cell, regrouped)
-    collision_term = lax.all_to_all(cell_terms, "vel", split_axis=1, concat_axis=0, tiled=True)
+    devices, mine = (lax.axis_size("vel"), lax.axis_index("vel"))
+    tiles = cut_along(cell_terms, 1, devices)
+    out = tiles
+    for step in range(1, devices):
+        target, source = ((mine + step) % devices, (mine - step) % devices)
+        sent = lax.dynamic_index_in_dim(tiles, target, 0)
+        theirs = lax.ppermute(
+            sent, "vel", [(i_2, (i_2 + step) % devices) for i_2 in range(devices)]
+        )
+        out = lax.dynamic_update_slice_in_dim(out, theirs, source, axis=0)
+    collision_term = laid_out(out, 0)
     offset = lax.axis_index("space") * cell_count
     padded = padded_2(distribution, (("space", 0),), 1)
     mirror = distribution.reshape(cell_count, planes_dev, points, points)[:, :, ::-1, :].reshape(

time: 423 us -> 427 us (level)
  starting transfers between devices: 14.2 us -> 22.8 us
  waiting for transfers between devices: 25.3 us -> 17.5 us
    ppermute x0 -> x7, waiting for transfers between devices: none -> 16.2 us  [body(): lax.ppermute(sent, 'vel', [(i_2, (i_2 + step) % devices) for i_2 in range...]
    all_to_all x1, waiting for transfers between devices: 14.4 us -> 1.33 us  [body(): lax.all_to_all(distribution, 'vel', split_axis=0, concat_axis=1, tiled=True)]
    ppermute x0 -> x7, starting transfers between devices: none -> 12 us  [body(): lax.ppermute(sent, 'vel', [(i_2, (i_2 + step) % devices) for i_2 in range...]
    all_to_all x1 -> x0, waiting for transfers between devices: 10.9 us -> none  [body(): lax.all_to_all(cell_terms, 'vel', split_axis=1, concat_axis=0, tiled=True)]
    all_to_all x1 -> x0, starting transfers between devices: 4.36 us -> none  [body(): lax.all_to_all(cell_terms, 'vel', split_axis=1, concat_axis=0, tiled=True)]
  transfers between devices with their start and end apart: 4 -> 10, of which waited for: 2 -> 6; matrix products, arithmetic and copies ran while one was open for 6% -> 87% of each run, Pallas kernels for 0% -> 0%
where the time goes in v1:
time: 427 us; the launch traced here: 421 us
  matrix products  196 us (46%)
  local copies, waits for them, and re-layouts  94.1 us (22%)
  other arithmetic  84.3 us (20%)
  starting transfers between devices  22.8 us (5%)
  waiting for transfers between devices  17.5 us (4%)
  loops' own time  4.48 us (1%)
    dot_general x48, matrix products, apply_table(): lax.dot_general(tensor, table, ((dims, tuple(range(len(dims)))), ((), ())...  196 us
    dot_general x16, local copies, waits for them, and re-layouts, apply_table(): lax.dot_general(tensor, table, ((dims, tuple(range(len(dims)))), ((), ())...  60.7 us
    sub x6, other arithmetic, packed(): joined_real = first_factor * real_part - second_factor * imag_part  58.4 us
    ppermute x7, waiting for transfers between devices, body(): lax.ppermute(sent, 'vel', [(i_2, (i_2 + step) % devices) for i_2 in range...  16.2 us
    div x1, other arithmetic, kernel_tables(): loss_total = sum(loss_tables) / 6.0  13.5 us
    ppermute x7, starting transfers between devices, body(): lax.ppermute(sent, 'vel', [(i_2, (i_2 + step) % devices) for i_2 in range...  12 us
  transfers between devices with their start and end apart: 10, of which 6 were waited for; matrix products, arithmetic and copies ran while one was open for 87% of the time, Pallas kernels for 0%

profile of v1, /device:TPU:0, one launch (start us, length us, event | category | flops | bytes accessed | tf_op | source)
XLA Modules:
  0.0 420.5 jit_solution(13772094419603681201)
XLA Ops:
  2.8 7.4 %all-to-all-start = ((f32[16,6,2304]{2,1,0:T(8,128)}), f32[16,6,2304]{2,1,0:T(8,128)}, u32[]{:S(2)}, u32[]{:S(2)}) async-start(f32[16,6,2304]{2,1,0:T(8,128)} %copy.84), calls=%async_computation | async-start | bytes 2359296 | tf_op jit(solution)/shard_map/all_to_all | solution.py:149
  23.9 13.5 %add_multiply_fusion = (f32[48,48,48]{2,1,0:T(8,128)}, f32[48,48,48]{2,1,0:T(8,128)}, f32[48,48,48]{2,1,0:T(8,128)}, f32[48,48,48]{2,1,0:T(8,128)}, f32[48,48,48...) fusion(f32[48]{0:T(128)S(1)} %get-tuple-element.744, f32[48,48]{1,0:T(8,128)S(1)} %get-tuple-element.746, ...), kind=kLoop, calls=%fused_computation.329 | loop fusion | flops 26652672 | bytes 3161856 | tf_op jit(solution)/shard_map/div | solution.py:70
  40.6 346.1 %while.13 = (s32[]{:T(128)}, f32[2,48,2304]{2,0,1:T(2,128)}, f32[2,48,2304]{2,0,1:T(2,128)S(1)}, f32[48,2,48]{2,0,1:T(8,128)S(1)}, f32[48,2,2,48]{3,0,1,2:T(8,12...) while((s32[]{:T(128)}, f32[2,48,2304]{2,0,1:T(2,128)}, ...), condition=%wide.region_1.3_spmd.clone.clone.clone, body=%wide.region_0.2_spmd.clone.clone.clone.sunk | while | flops 5998288896 | bytes 128030208 | solution.py:150
  50.4 6.0 %fusion.365 = f32[48,48,2,48,1]{0,3,4,2,1:T(8,128)S(1)} fusion(f32[48,48,2,48,1]{1,0,2,4,3:T(8,128)} %copy.177, f32[48,2,2,48]{3,0,1,2:T(8,128)S(1)} %get-tuple-element.777), kind=kOutput, calls=%fused_computation.156.clone.1 | convolution fusion | flops 254803968 | bytes 1806336 | tf_op jit(solution)/shard_map/while/body/eval_jaxpr/dot_general | solution.py:91
  58.5 9.9 %fusion.367 = (f32[48,48,1,48]{3,1,2,0:T(8,128)}, f32[48,48,1,48]{3,1,2,0:T(8,128)}, f32[48,48,1,48]{3,1,2,0:T(8,128)S(1)}, f32[48,48,1,48]{3,1,2,0:T(8,128)S(1)...) fusion(f32[48,48,48]{2,1,0:T(8,128)S(1)} %copy-done.16, f32[48]{0:T(128)S(1)} %get-tuple-element.786, ...), kind=kLoop, calls=%fused_computation.117.clone.1 | loop fusion | flops 2211840 | bytes 4884672 | tf_op jit(solution)/shard_map/while/body/eval_jaxpr/sub | solution.py:122
  75.9 6.0 %fusion.381 = f32[48,48,2,48,1]{0,3,4,2,1:T(8,128)S(1)} fusion(f32[48,48,2,48,1]{0,1,2,4,3:T(8,128)} %copy.183, f32[48,2,2,48]{3,0,1,2:T(8,128)S(1)} %get-tuple-element.779), kind=kOutput, calls=%fused_computation.148.clone.1 | convolution fusion | flops 254803968 | bytes 1806336 | tf_op jit(solution)/shard_map/while/body/eval_jaxpr/dot_general | solution.py:91
  92.9 6.0 %fusion.383 = f32[48,48,2,48,1]{0,3,4,2,1:T(8,128)S(1)} fusion(f32[48,48,2,48,1]{0,1,2,4,3:T(8,128)} %copy.184, f32[48,2,2,48]{3,0,1,2:T(8,128)S(1)} %get-tuple-element.779), kind=kOutput, calls=%fused_computation.152.clone.1 | convolution fusion | flops 254803968 | bytes 1806336 | tf_op jit(solution)/shard_map/while/body/eval_jaxpr/dot_general | solution.py:91
  102.4 9.6 %fusion.370 = (f32[48,48,1,48]{3,1,2,0:T(8,128)}, f32[48,48,1,48]{3,1,2,0:T(8,128)}, f32[48,48,1,48]{3,1,2,0:T(8,128)S(1)}, f32[48,48,1,48]{3,1,2,0:T(8,128)S(1)}) fusion(f32[48,48,48]{2,1,0:T(8,128)S(1)} %copy-done.18, f32[48]{0:T(128)S(1)} %get-tuple-element.792, f32[48,48]{1,0:T(8,128)S(1)} %copy-done.28, f32[48,48,2,48]{3,1,2,0:T(8,128)S(1)} %fusion.366, ...), kind=kLoop, calls=%fused_computation.93.clone.1 | loop fusion | flops 1769472 | bytes 3557568 | tf_op jit(solution)/shard_map/while/body/eval_jaxpr/sub | solution.py:122
  119.6 6.0 %fusion.372 = f32[48,48,2,48,1]{0,3,4,2,1:T(8,128)S(1)} fusion(f32[48,48,2,48,1]{0,1,2,4,3:T(8,128)} %copy.179, f32[48,2,2,48]{3,0,1,2:T(8,128)S(1)} %get-tuple-element.779), kind=kOutput, calls=%fused_computation.132.clone.1 | convolution fusion | flops 254803968 | bytes 1806336 | tf_op jit(solution)/shard_map/while/body/eval_jaxpr/dot_general | solution.py:91
  132.6 4.1 copy.180
  136.8 6.0 %fusion.374 = f32[48,48,2,48,1]{0,3,4,2,1:T(8,128)S(1)} fusion(f32[48,48,2,48,1]{0,1,2,4,3:T(8,128)} %copy.180, f32[48,2,2,48]{3,0,1,2:T(8,128)S(1)} %get-tuple-element.779), kind=kOutput, calls=%fused_computation.136.clone.1 | convolution fusion | flops 254803968 | bytes 1806336 | tf_op jit(solution)/shard_map/while/body/eval_jaxpr/dot_general | solution.py:91
  146.4 9.6 %fusion.375 = (f32[48,48,1,48]{3,1,2,0:T(8,128)}, f32[48,48,1,48]{3,1,2,0:T(8,128)}, f32[48,48,1,48]{3,1,2,0:T(8,128)S(1)}, f32[48,48,1,48]{3,1,2,0:T(8,128)S(1)}) fusion(f32[48,48,48]{2,1,0:T(8,128)S(1)} %copy-done.14, f32[48]{0:T(128)S(1)} %get-tuple-element.789, f32[48,48]{1,0:T(8,128)S(1)} %copy-done.30, f32[48,48,2,48]{3,1,2,0:T(8,128)S(1)} %fusion.366, ...), kind=kLoop, calls=%fused_computation.105.clone.1 | loop fusion | flops 1769472 | bytes 3557568 | tf_op jit(solution)/shard_map/while/body/eval_jaxpr/sub | solution.py:122
  160.8 6.0 %fusion.377 = f32[48,48,2,48,1]{0,3,4,2,1:T(8,128)S(1)} fusion(f32[48,48,2,48,1]{0,1,2,4,3:T(8,128)} %copy.181, f32[48,2,2,48]{3,0,1,2:T(8,128)S(1)} %get-tuple-element.779), kind=kOutput, calls=%fused_computation.140.clone.1 | convolution fusion | flops 254803968 | bytes 1806336 | tf_op jit(solution)/shard_map/while/body/eval_jaxpr/dot_general | solution.py:91
  176.3 6.0 %fusion.379 = f32[48,48,2,48,1]{0,3,4,2,1:T(8,128)S(1)} fusion(f32[48,48,2,48,1]{0,1,2,4,3:T(8,128)} %copy.182, f32[48,2,2,48]{3,0,1,2:T(8,128)S(1)} %get-tuple-element.779), kind=kOutput, calls=%fused_computation.144.clone.1 | convolution fusion | flops 254803968 | bytes 1806336 | tf_op jit(solution)/shard_map/while/body/eval_jaxpr/dot_general | solution.py:91
  193.2 6.2 %fusion.369 = f32[48,48,2,48,1]{0,3,4,2,1:T(8,128)S(1)} fusion(f32[48,48,2,48,1]{0,1,2,4,3:T(8,128)} %copy.178, f32[48,2,2,48]{3,0,1,2:T(8,128)S(1)} %get-tuple-element.779), kind=kOutput, calls=%fused_computation.128.clone.1 | convolution fusion | flops 254803968 | bytes 1806336 | tf_op jit(solution)/shard_map/while/body/eval_jaxpr/dot_general | solution.py:91
  201.8 4.1 fusion.384
  221.9 6.0 %fusion.365 = f32[48,48,2,48,1]{0,3,4,2,1:T(8,128)S(1)} fusion(f32[48,48,2,48,1]{1,0,2,4,3:T(8,128)} %copy.177, f32[48,2,2,48]{3,0,1,2:T(8,128)S(1)} %get-tuple-element.777), kind=kOutput, calls=%fused_computation.156.clone.1 | convolution fusion | flops 254803968 | bytes 1806336 | tf_op jit(solution)/shard_map/while/body/eval_jaxpr/dot_general | solution.py:91
  230.0 9.9 %fusion.367 = (f32[48,48,1,48]{3,1,2,0:T(8,128)}, f32[48,48,1,48]{3,1,2,0:T(8,128)}, f32[48,48,1,48]{3,1,2,0:T(8,128)S(1)}, f32[48,48,1,48]{3,1,2,0:T(8,128)S(1)...) fusion(f32[48,48,48]{2,1,0:T(8,128)S(1)} %copy-done.16, f32[48]{0:T(128)S(1)} %get-tuple-element.786, ...), kind=kLoop, calls=%fused_computation.117.clone.1 | loop fusion | flops 2211840 | bytes 4884672 | tf_op jit(solution)/shard_map/while/body/eval_jaxpr/sub | solution.py:122
  247.4 6.0 %fusion.381 = f32[48,48,2,48,1]{0,3,4,2,1:T(8,128)S(1)} fusion(f32[48,48,2,48,1]{0,1,2,4,3:T(8,128)} %copy.183, f32[48,2,2,48]{3,0,1,2:T(8,128)S(1)} %get-tuple-element.779), kind=kOutput, calls=%fused_computation.148.clone.1 | convolution fusion | flops 254803968 | bytes 1806336 | tf_op jit(solution)/shard_map/while/body/eval_jaxpr/dot_general | solution.py:91
  264.4 6.0 %fusion.383 = f32[48,48,2,48,1]{0,3,4,2,1:T(8,128)S(1)} fusion(f32[48,48,2,48,1]{0,1,2,4,3:T(8,128)} %copy.184, f32[48,2,2,48]{3,0,1,2:T(8,128)S(1)} %get-tuple-element.779), kind=kOutput, calls=%fused_computation.152.clone.1 | convolution fusion | flops 254803968 | bytes 1806336 | tf_op jit(solution)/shard_map/while/body/eval_jaxpr/dot_general | solution.py:91
  274.0 9.6 %fusion.370 = (f32[48,48,1,48]{3,1,2,0:T(8,128)}, f32[48,48,1,48]{3,1,2,0:T(8,128)}, f32[48,48,1,48]{3,1,2,0:T(8,128)S(1)}, f32[48,48,1,48]{3,1,2,0:T(8,128)S(1)}) fusion(f32[48,48,48]{2,1,0:T(8,128)S(1)} %copy-done.18, f32[48]{0:T(128)S(1)} %get-tuple-element.792, f32[48,48]{1,0:T(8,128)S(1)} %copy-done.28, f32[48,48,2,48]{3,1,2,0:T(8,128)S(1)} %fusion.366, ...), kind=kLoop, calls=%fused_computation.93.clone.1 | loop fusion | flops 1769472 | bytes 3557568 | tf_op jit(solution)/shard_map/while/body/eval_jaxpr/sub | solution.py:122
  287.1 4.3 %copy.179 = f32[48,48,2,48,1]{0,1,2,4,3:T(8,128)} copy(f32[48,48,2,48,1]{3,1,2,0,4:T(8,128)} %fusion.371) | data formatting | bytes 1769472 | tf_op jit(solution)/shard_map/while/body/eval_jaxpr/dot_general | solution.py:91
  291.3 6.0 %fusion.372 = f32[48,48,2,48,1]{0,3,4,2,1:T(8,128)S(1)} fusion(f32[48,48,2,48,1]{0,1,2,4,3:T(8,128)} %copy.179, f32[48,2,2,48]{3,0,1,2:T(8,128)S(1)} %get-tuple-element.779), kind=kOutput, calls=%fused_computation.132.clone.1 | convolution fusion | flops 254803968 | bytes 1806336 | tf_op jit(solution)/shard_map/while/body/eval_jaxpr/dot_general | solution.py:91
  308.2 6.0 %fusion.374 = f32[48,48,2,48,1]{0,3,4,2,1:T(8,128)S(1)} fusion(f32[48,48,2,48,1]{0,1,2,4,3:T(8,128)} %copy.180, f32[48,2,2,48]{3,0,1,2:T(8,128)S(1)} %get-tuple-element.779), kind=kOutput, calls=%fused_computation.136.clone.1 | convolution fusion | flops 254803968 | bytes 1806336 | tf_op jit(solution)/shard_map/while/body/eval_jaxpr/dot_general | solution.py:91
  317.9 9.6 %fusion.375 = (f32[48,48,1,48]{3,1,2,0:T(8,128)}, f32[48,48,1,48]{3,1,2,0:T(8,128)}, f32[48,48,1,48]{3,1,2,0:T(8,128)S(1)}, f32[48,48,1,48]{3,1,2,0:T(8,128)S(1)}) fusion(f32[48,48,48]{2,1,0:T(8,128)S(1)} %copy-done.14, f32[48]{0:T(128)S(1)} %get-tuple-element.789, f32[48,48]{1,0:T(8,128)S(1)} %copy-done.30, f32[48,48,2,48]{3,1,2,0:T(8,128)S(1)} %fusion.366, ...), kind=kLoop, calls=%fused_computation.105.clone.1 | loop fusion | flops 1769472 | bytes 3557568 | tf_op jit(solution)/shard_map/while/body/eval_jaxpr/sub | solution.py:122
  332.3 6.0 %fusion.377 = f32[48,48,2,48,1]{0,3,4,2,1:T(8,128)S(1)} fusion(f32[48,48,2,48,1]{0,1,2,4,3:T(8,128)} %copy.181, f32[48,2,2,48]{3,0,1,2:T(8,128)S(1)} %get-tuple-element.779), kind=kOutput, calls=%fused_computation.140.clone.1 | convolution fusion | flops 254803968 | bytes 1806336 | tf_op jit(solution)/shard_map/while/body/eval_jaxpr/dot_general | solution.py:91
  347.9 6.0 %fusion.379 = f32[48,48,2,48,1]{0,3,4,2,1:T(8,128)S(1)} fusion(f32[48,48,2,48,1]{0,1,2,4,3:T(8,128)} %copy.182, f32[48,2,2,48]{3,0,1,2:T(8,128)S(1)} %get-tuple-element.779), kind=kOutput, calls=%fused_computation.144.clone.1 | convolution fusion | flops 254803968 | bytes 1806336 | tf_op jit(solution)/shard_map/while/body/eval_jaxpr/dot_general | solution.py:91
  364.8 6.2 %fusion.369 = f32[48,48,2,48,1]{0,3,4,2,1:T(8,128)S(1)} fusion(f32[48,48,2,48,1]{0,1,2,4,3:T(8,128)} %copy.178, f32[48,2,2,48]{3,0,1,2:T(8,128)S(1)} %get-tuple-element.779), kind=kOutput, calls=%fused_computation.128.clone.1 | convolution fusion | flops 254803968 | bytes 1806336 | tf_op jit(solution)/shard_map/while/body/eval_jaxpr/dot_general | solution.py:91
  373.4 4.1 fusion.384
  392.5 4.2 collective-permute-done.2
  397.9 8.2 %collective-permute-done.4 = f32[1,2,6,2304]{3,1,2,0:T(2,128)S(1)} collective-permute-done((f32[1,2,6,2304]{3,1,2,0:T(2,128)S(1)}, f32[1,2,6,2304]{3,1,2,0:T(2,128)S(1)}, u32[]{:S(2)}, u32[]{:S(2)}) %collective-permute-start.4) | collective-permute-done | bytes 110624 | tf_op jit(solution)/shard_map/ppermute | solution.py:157
  406.1 4.5 %collective-permute-start.7 = (f32[1,2,6,2304]{3,1,2,0:T(2,128)S(1)}, f32[1,2,6,2304]{3,1,2,0:T(2,128)S(1)}, u32[]{:S(2)}, u32[]{:S(2)}) collective-permute-start(f32[1,2,6,2304]{3,1,2,0:T(2,128)S(1)} %get-tuple-element.524), channel_id=1, source_target_pairs={{0,6},{1,7},{2,0},{3,1},{4,2},{5,3},{6,4},{7,5},{8,14},{9,15},{10,... | collective-permute-start | bytes 331784 | tf_op jit(solution)/shard_map/ppermute | solution.py:157
  (230 shorter events, 205.8 us)
Async XLA Ops:
  2.7 7.4 %copy-start.19 = (f32[16,6,2304]{2,0,1:T(8,128)S(1)}, f32[16,6,2304]{2,0,1:T(8,128)}, u32[]{:S(2)}) copy-start(f32[16,6,2304]{2,0,1:T(8,128)} %param.6) | copy-start | bytes 2654212
  2.8 36.1 %all-to-all-start = ((f32[16,6,2304]{2,1,0:T(8,128)}), f32[16,6,2304]{2,1,0:T(8,128)}, u32[]{:S(2)}, u32[]{:S(2)}) async-start(f32[16,6,2304]{2,1,0:T(8,128)} %copy.84), calls=%async_computation | async-start | bytes 2359296 | tf_op jit(solution)/shard_map/all_to_all | solution.py:149
  10.9 406.3 %collective-permute-start = (f32[1,6,2304]{2,0,1:T(1,128)}, f32[1,6,2304]{2,0,1:T(1,128)}, u32[]{:S(2)}, u32[]{:S(2)}) collective-permute-start(f32[1,6,2304]{2,0,1:T(1,128)} %get-tuple-element.530), channel_id=1, source_target_pairs={{0,8},{8,16},{16,24},{1,9},{9,17},{17,25},{2,10},{10,18},{18,26},{... | collective-permute-start | bytes 165896 | tf_op jit(solution)/shard_map/ppermute | solution.py:43
  12.9 404.3 %collective-permute-start.1 = (f32[1,6,2304]{2,0,1:T(1,128)}, f32[1,6,2304]{2,0,1:T(1,128)}, u32[]{:S(2)}, u32[]{:S(2)}) collective-permute-start(f32[1,6,2304]{2,0,1:T(1,128)} %get-tuple-element.531), channel_id=1, source_target_pairs={{8,0},{16,8},{24,16},{9,1},{17,9},{25,17},{10,2},{18,10},{26,18},{... | collective-permute-start | bytes 165896 | tf_op jit(solution)/shard_map/ppermute | solution.py:45
  14.2 9.7 %copy-start.34 = (f32[48]{0:T(128)}, f32[48]{0:T(128)S(1)}, u32[]{:S(2)}) copy-start(f32[48]{0:T(128)S(1)} %get-tuple-element.741) | copy-start | bytes 580
  23.9 13.6 %copy-start.25 = (f32[48,48]{1,0:T(8,128)}, f32[48,48]{1,0:T(8,128)S(1)}, u32[]{:S(2)}) copy-start(f32[48,48]{1,0:T(8,128)S(1)} %get-tuple-element.743) | copy-start | bytes 27652
  23.9 13.6 %copy-start.27 = (f32[48,48]{1,0:T(8,128)}, f32[48,48]{1,0:T(8,128)S(1)}, u32[]{:S(2)}) copy-start(f32[48,48]{1,0:T(8,128)S(1)} %get-tuple-element.745) | copy-start | bytes 27652
  23.9 13.6 %copy-start.29 = (f32[48,48]{1,0:T(8,128)}, f32[48,48]{1,0:T(8,128)S(1)}, u32[]{:S(2)}) copy-start(f32[48,48]{1,0:T(8,128)S(1)} %get-tuple-element.742) | copy-start | bytes 27652
  23.9 13.6 %copy-start.31 = (f32[48,48]{1,0:T(8,128)}, f32[48,48]{1,0:T(8,128)S(1)}, u32[]{:S(2)}) copy-start(f32[48,48]{1,0:T(8,128)S(1)} %get-tuple-element.739) | copy-start | bytes 27652
  98.9 3.6 copy-start.17
  98.9 3.6 copy-start.18
  142.8 3.6 copy-start.13
  142.8 3.6 copy-start.14
  142.8 3.6 copy-start.26
  142.8 3.6 copy-start.30
  193.2 8.3 %copy-start.2 = (f32[48,48,2,48]{3,1,2,0:T(8,128)S(1)}, f32[48,48,2,48]{3,1,2,0:T(8,128)}, u32[]{:S(2)}) copy-start(f32[48,48,2,48]{3,1,2,0:T(8,128)} %bitcast_multiply_fusion.41) | copy-start | bytes 2654212 | tf_op jit(solution)/shard_map/while
  193.2 8.3 %copy-start.3 = (f32[48,48,2,48]{3,1,2,0:T(8,128)S(1)}, f32[48,48,2,48]{3,1,2,0:T(8,128)}, u32[]{:S(2)}) copy-start(f32[48,48,2,48]{3,1,2,0:T(8,128)} %bitcast_multiply_fusion.42) | copy-start | bytes 2654212 | tf_op jit(solution)/shard_map/while
  270.4 3.6 copy-start.17
  314.2 3.6 copy-start.13
  314.3 3.6 copy-start.14
  314.3 3.6 copy-start.26
  314.3 3.6 copy-start.30
  364.8 8.3 %copy-start.2 = (f32[48,48,2,48]{3,1,2,0:T(8,128)S(1)}, f32[48,48,2,48]{3,1,2,0:T(8,128)}, u32[]{:S(2)}) copy-start(f32[48,48,2,48]{3,1,2,0:T(8,128)} %bitcast_multiply_fusion.41) | copy-start | bytes 2654212 | tf_op jit(solution)/shard_map/while
  364.8 8.3 %copy-start.3 = (f32[48,48,2,48]{3,1,2,0:T(8,128)S(1)}, f32[48,48,2,48]{3,1,2,0:T(8,128)}, u32[]{:S(2)}) copy-start(f32[48,48,2,48]{3,1,2,0:T(8,128)} %bitcast_multiply_fusion.42) | copy-start | bytes 2654212 | tf_op jit(solution)/shard_map/while
  386.6 10.0 %copy-start.24 = (f32[2,48,2304]{2,0,1:T(2,128)S(1)}, f32[2,48,2304]{2,0,1:T(2,128)}, u32[]{:S(2)}) copy-start(f32[2,48,2304]{2,0,1:T(2,128)} %get-tuple-element.142) | copy-start | bytes 2654212
  388.0 8.7 %collective-permute-start.2 = (f32[1,2,6,2304]{3,1,2,0:T(2,128)S(1)}, f32[1,2,6,2304]{3,1,2,0:T(2,128)S(1)}, u32[]{:S(2)}, u32[]{:S(2)}) collective-permute-start(f32[1,2,6,2304]{3,1,2,0:T(2,128)S(1)} %get-tuple-element.529), channel_id=1, source_target_pairs={{0,1},{1,2},{2,3},{3,4},{4,5},{5,6},{6,7},{7,0},{8,9},{9,10},{10,1... | collective-permute-start | bytes 331784 | tf_op jit(solution)/shard_map/ppermute | solution.py:157
  389.5 7.6 %collective-permute-start.3 = (f32[1,2,6,2304]{3,1,2,0:T(2,128)S(1)}, f32[1,2,6,2304]{3,1,2,0:T(2,128)S(1)}, u32[]{:S(2)}, u32[]{:S(2)}) collective-permute-start(f32[1,2,6,2304]{3,1,2,0:T(2,128)S(1)} %get-tuple-element.528), channel_id=1, source_target_pairs={{0,2},{1,3},{2,4},{3,5},{4,6},{5,7},{6,0},{7,1},{8,10},{9,11},{10,... | collective-permute-start | bytes 331784 | tf_op jit(solution)/shard_map/ppermute | solution.py:157
  390.1 16.0 %collective-permute-start.4 = (f32[1,2,6,2304]{3,1,2,0:T(2,128)S(1)}, f32[1,2,6,2304]{3,1,2,0:T(2,128)S(1)}, u32[]{:S(2)}, u32[]{:S(2)}) collective-permute-start(f32[1,2,6,2304]{3,1,2,0:T(2,128)S(1)} %get-tuple-element.527), channel_id=1, source_target_pairs={{0,3},{1,4},{2,5},{3,6},{4,7},{5,0},{6,1},{7,2},{8,11},{9,12},{10,... | collective-permute-start | bytes 331784 | tf_op jit(solution)/shard_map/ppermute | solution.py:157
  396.7 14.0 %collective-permute-start.5 = (f32[1,2,6,2304]{3,1,2,0:T(2,128)S(1)}, f32[1,2,6,2304]{3,1,2,0:T(2,128)S(1)}, u32[]{:S(2)}, u32[]{:S(2)}) collective-permute-start(f32[1,2,6,2304]{3,1,2,0:T(2,128)S(1)} %get-tuple-element.526), channel_id=1, source_target_pairs={{0,4},{1,5},{2,6},{3,7},{4,0},{5,1},{6,2},{7,3},{8,12},{9,13},{10,... | collective-permute-start | bytes 331784 | tf_op jit(solution)/shard_map/ppermute | solution.py:157
  397.1 15.9 %collective-permute-start.6 = (f32[1,2,6,2304]{3,1,2,0:T(2,128)S(1)}, f32[1,2,6,2304]{3,1,2,0:T(2,128)S(1)}, u32[]{:S(2)}, u32[]{:S(2)}) collective-permute-start(f32[1,2,6,2304]{3,1,2,0:T(2,128)S(1)} %get-tuple-element.525), channel_id=1, source_target_pairs={{0,5},{1,6},{2,7},{3,0},{4,1},{5,2},{6,3},{7,4},{8,13},{9,14},{10,... | collective-permute-start | bytes 331784 | tf_op jit(solution)/shard_map/ppermute | solution.py:157
  406.1 7.2 %collective-permute-start.7 = (f32[1,2,6,2304]{3,1,2,0:T(2,128)S(1)}, f32[1,2,6,2304]{3,1,2,0:T(2,128)S(1)}, u32[]{:S(2)}, u32[]{:S(2)}) collective-permute-start(f32[1,2,6,2304]{3,1,2,0:T(2,128)S(1)} %get-tuple-element.524), channel_id=1, source_target_pairs={{0,6},{1,7},{2,0},{3,1},{4,2},{5,3},{6,4},{7,5},{8,14},{9,15},{10,... | collective-permute-start | bytes 331784 | tf_op jit(solution)/shard_map/ppermute | solution.py:157
  410.6 5.8 %collective-permute-start.8 = (f32[1,2,6,2304]{3,1,2,0:T(2,128)S(1)}, f32[1,2,6,2304]{3,1,2,0:T(2,128)S(1)}, u32[]{:S(2)}, u32[]{:S(2)}) collective-permute-start(f32[1,2,6,2304]{3,1,2,0:T(2,128)S(1)} %get-tuple-element.523), channel_id=1, source_target_pairs={{0,7},{1,0},{2,1},{3,2},{4,3},{5,4},{6,5},{7,6},{8,15},{9,8},{10,9... | collective-permute-start | bytes 331784 | tf_op jit(solution)/shard_map/ppermute | solution.py:157
  (40 other events, 102.2 us)
